TPU v7x, 256 devices: a whole 4x4x8 slice. The times are simulated.
256 devices in a mesh: sym: 8 (over y, core), rows: 32 (over z, x).
Axes of the slice: x: 4, y: 4, z: 8, core: 2. Of those that a mesh axis runs over, the one named last changes fastest.
Arguments:
- coeffs: bfloat16 [16384, 8192], P('rows', 'sym'), may hold values from -6 to 6
- beta_op: bfloat16 [8, 1024, 1024], P('sym'), may hold values from -0.1875 to 0.1875
- mix_op: bfloat16 [8, 8, 8, 128, 128], P('sym'), may hold values from -0.125 to 0.125
- pair_op: bfloat16 [8, 128, 128], replicated, may hold values from -0.1875 to 0.1875
- send_list: int32 [32, 32, 2], replicated, may hold values from -1 to 3, as said below
- mix_slot: int32 [128, 16], replicated, may hold values from 0 to 63, as said below
- mix_sign: int32 [128, 16], replicated, may hold values from 0 to 1
- mix_pair: int32 [128, 16], replicated, may hold values from 0 to 7
- aa_src: int32 [128, 8], replicated, may hold values from 0 to 127
- aa_sign: int32 [128, 8], replicated, may hold values from 0 to 1
- aa_pair: int32 [128, 8], replicated, may hold values from 0 to 7
Outputs:
- sigma: float32 [16384, 8192], P('rows', 'sym')
Inputs may be any that keep to these rules, and one draw needn't show every extreme that they name: send_list[s, r, c] is the block, counted within device s's own 4 alpha blocks, that s sends to device r in slot c, or -1 for an empty slot; live slots of a pair come first and hold distinct blocks; every device sends at least one block to itself; in every draw some device receives 2 blocks from every device. mix_slot[P, l] = s * 2 + c names slot c of send_list[s, P // 4], always a live one; every live slot sent to a device is named by some entry of that device's destination blocks.
All inputs are finite; a program needn't handle non-finite values.
Results may differ from a plain program's by a relative error of at most 0.0075.
Values may be sent and summed in bfloat16 or wider, within the bound.
No kernel may reach another device: no remote copies, remote signals or barrier semaphores. Data moves between devices by JAX's collectives and lax.ppermute only.
A program may use at most 128 MiB of HBM per device.

v0:
```python
import jax
import jax.numpy as jnp
from jax import lax
from jax.sharding import PartitionSpec as P

TILE = 128
BT = 8
ABLK = 4
CAP = 2
NPA = 8


def cut_along(array, dim, devices):
    dims = array.shape
    parts = array.reshape(*dims[:dim], devices, dims[dim] // devices, *dims[dim + 1 :])
    return jnp.moveaxis(parts, dim, 0)


def piece_ends(length, count):
    hop = length // count
    if hop >= 8:
        hop -= hop % 8
    return [hop * k for k in range(1, count)]


def laid_out(parts, dim):
    dims = list(parts.shape[1:])
    dims[dim] *= parts.shape[0]
    return jnp.moveaxis(parts, 0, dim).reshape(dims)


def exchange_in_pieces(array, axis, pieces, split_dim, concat_dim):
    parts = cut_along(array, split_dim, lax.axis_size(axis))
    widest = max(range(1, max(2, parts.ndim - 1)), key=lambda d: parts.shape[d])
    finished = []
    for slab in jnp.split(parts, piece_ends(parts.shape[widest], pieces), axis=widest):
        if slab.size:
            finished.append(lax.all_to_all(slab, axis, split_axis=0, concat_axis=0, tiled=True))
    return laid_out(jnp.concatenate(finished, axis=widest), concat_dim)


def per_device(
    coeffs,
    beta_op,
    mix_op,
    pair_op,
    send_list,
    mix_slot,
    mix_sign,
    mix_pair,
    aa_src,
    aa_sign,
    aa_pair,
):
    rows_here, beta_here = coeffs.shape
    sectors = lax.axis_size("sym")
    rank_count = lax.axis_size("rows")
    sector = lax.axis_index("sym")
    block_count = aa_src.shape[0]
    total_rows = block_count * TILE
    col_width = beta_here // rank_count
    local_term = jnp.dot(coeffs, beta_op[0], preferred_element_type=jnp.float32)
    flipped = coeffs.T
    columns = lax.all_to_all(flipped, "rows", split_axis=0, concat_axis=1, tiled=True)
    col_blocks = columns.reshape(col_width, block_count, TILE)
    picked = jnp.take(col_blocks, aa_src, axis=1)
    operator_ids = jnp.arange(NPA, dtype=jnp.int32)
    aa_weight = (
        (1 - 2 * aa_sign)[:, :, None]
        * (aa_pair[:, :, None] == operator_ids[None, None, :]).astype(jnp.int32)
    ).astype(jnp.bfloat16)
    combined = jnp.einsum(
        "cpki,pkg->cpgi", picked, aa_weight, preferred_element_type=jnp.float32
    ).astype(jnp.bfloat16)
    alpha_part = jnp.einsum(
        "cpgj,gij->cpi", combined, pair_op, preferred_element_type=jnp.float32
    ).reshape(col_width, total_rows)
    returned = lax.all_to_all(
        alpha_part.astype(jnp.bfloat16), "rows", split_axis=1, concat_axis=0, tiled=True
    ).astype(alpha_part.dtype)
    dest_ids = jnp.arange(sectors, dtype=jnp.int32)
    pair_of = jnp.bitwise_xor(sector, dest_ids)
    operators = jnp.take(mix_op[0], pair_of, axis=0)
    sign_all = (1 - 2 * mix_sign).astype(jnp.float32)
    slot_src = mix_slot // CAP
    slot_pos = mix_slot % CAP
    dest_rank = (jnp.arange(block_count, dtype=jnp.int32) // ABLK)[:, None]
    owned_blk = send_list[slot_src, dest_rank, slot_pos]
    source = slot_src * ABLK + owned_blk
    gathered = jnp.take(col_blocks, source, axis=1)
    mix_weight = (
        sign_all[None, :, :] * (mix_pair[None, :, :] == pair_of[:, None, None]).astype(jnp.float32)
    ).astype(jnp.bfloat16)
    combos = jnp.einsum(
        "cpli,dpl->dcpi", gathered, mix_weight, preferred_element_type=jnp.float32
    ).astype(jnp.bfloat16)
    combos = combos.reshape(sectors, col_width, total_rows)
    came_back = exchange_in_pieces(combos, "rows", 2, 2, 1)
    inputs = came_back.reshape(sectors, BT, TILE, rows_here)
    contract_eq = "dtkr,dtkj->drtj"
    row_count = lax.axis_size("sym") * rows_here
    products = jnp.einsum(contract_eq, inputs, operators, preferred_element_type=jnp.float32)
    mixed = lax.psum_scatter(
        products.reshape(row_count, beta_here).astype(jnp.bfloat16),
        "sym",
        scatter_dimension=0,
        tiled=True,
    ).astype(jnp.float32)
    return local_term + returned.T + mixed


def solution(mesh):
    in_specs = (
        P("rows", "sym"),
        P("sym", None, None),
        P("sym", None, None, None, None),
        P(),
        P(),
        P(),
        P(),
        P(),
        P(),
        P(),
        P(),
    )
    out_specs = P("rows", "sym")
    return jax.shard_map(
        per_device, mesh=mesh, in_specs=in_specs, out_specs=out_specs, check_vma=False
    )
```

profile of v0, /device:TPU:18, one launch (start us, length us, event | category | flops | bytes accessed | tf_op | source)
XLA Modules:
  0.0 472.6 jit_solution(12893267071110367578)
XLA Ops:
  6.5 0.0 copy-start
  6.5 2.4 copy.74
  9.0 11.6 %all-to-all-start = ((bf16[32,32,512]{2,1,0:T(8,128)(2,1)}), bf16[32,32,512]{2,1,0:T(8,128)(2,1)S(1)}, u32[]{:S(2)}, u32[]{:S(2)}) async-start(bf16[32,32,512]{2,1,0:T(8,128)(2,1)} %bitcast.84), calls=%async_computation | async-start | bytes 2097152 | tf_op jit(solution)/shard_map/all_to_all | solution.py:64
  20.6 0.7 fusion.38
  21.3 0.1 copy.84
  21.4 0.1 reshape.96
  21.5 0.0 copy-done.1
  21.5 0.0 copy-start.4
  21.5 0.0 copy-start.6
  21.5 0.0 copy-start.7
  21.5 20.1 %gather_fusion.2 = s32[2048]{0:T(1024)S(1)} fusion(s32[32,32,2]{1,2,0:T(2,128)S(1)} %copy-done.1, s32[2048]{0:T(1024)S(1)} %reshape.96), kind=kCustom, calls=%fused_computation.2 | custom fusion | bytes 40960 | tf_op jit(solution)/shard_map/gather | solution.py:88
  41.7 0.1 reshape.99
  41.7 0.1 copy.85
  41.8 0.0 copy-done.4
  41.8 0.1 copy.87
  41.9 0.1 reshape.104
  42.0 0.1 copy.86
  42.2 0.0 copy-done.6
  42.2 0.1 copy.82
  42.3 0.0 copy-done.7
  42.3 0.1 copy.83
  42.4 6.2 %all-to-all-done = bf16[32,32,512]{2,1,0:T(8,128)(2,1)S(1)} async-done(((bf16[32,32,512]{2,1,0:T(8,128)(2,1)}), bf16[32,32,512]{2,1,0:T(8,128)(2,1)S(1)}, u32[]{:S(2)}, u32[]{:S(2)}) %all-to-all-start) | async-done | bytes 1048608 | tf_op jit(solution)/shard_map/all_to_all | solution.py:64
  48.7 1.5 copy.75
  50.2 2.5 reshape.78
  52.7 1.9 copy.77
  54.6 19.2 %gather_fusion.3 = bf16[2048,32,128]{2,1,0:T(8,128)(2,1)} fusion(bf16[32,128,128]{2,0,1:T(8,128)(2,1)S(1)} %copy.77, s32[2048]{0:T(1024)S(1)} %broadcast_clamp_fusion), kind=kCustom, calls=%fused_computation.3 | custom fusion | bytes 33562624 | tf_op jit(solution)/shard_map/jit(_take)/gather | solution.py:90
  73.8 14.4 %select_bitcast_fusion = bf16[32,128,16,128]{3,0,2,1:T(8,128)(2,1)} fusion(bf16[128,16,32,128]{3,2,1,0:T(8,128)(2,1)} %bitcast.76, pred[128,16]{1,0:T(8,128)(4,1)S(1)} %copy.86), kind=kLoop, calls=%fused_computation.6 | loop fusion | flops 8388608 | bytes 33556480 | tf_op jit(solution)/shard_map/jit(_take)/select_n | solution.py:90
  88.2 25.9 %convert_bitcast_fusion.1 = bf16[8,32,128,128]{3,0,1,2:T(8,128)(2,1)} fusion(bf16[32,128,16,128]{3,0,2,1:T(8,128)(2,1)} %select_bitcast_fusion, bf16[128,16]{1,0:T(8,128)(2,1)S(1)} %copy.83, s32[128,16]{1,0:T(8,128)S(1)} %copy.82, s32[8]{0:T(128)S(1)} %iota_xor_fusion), kind=kOutput, calls=%fused_computation.15 | convolution fusion | flops 138444800 | bytes 25178144 | tf_op jit(solution)/shard_map/cpli,dpl->dcpi/dot_general | solution.py:94
  114.1 12.0 %copy.90 = bf16[8,32,128,128]{3,2,1,0:T(8,128)(2,1)} copy(bf16[8,32,128,128]{3,0,1,2:T(8,128)(2,1)} %convert_bitcast_fusion.1) | data formatting | bytes 16777216 | tf_op jit(solution)/shard_map/convert_element_type | solution.py:96
  126.1 14.0 %reshape_reshape.6 = bf16[8,32,32,512]{3,2,1,0:T(8,128)(2,1)} reshape(bf16[8,32,128,128]{3,2,1,0:T(8,128)(2,1)} %copy.90) | data formatting | bytes 16777216 | tf_op jit(solution)/shard_map/reshape;reshape | solution.py:15
  140.1 5.3 %fusion.51 = (bf16[32,8,16,512]{3,0,2,1:T(8,128)(2,1)S(1)}, bf16[32,8,16,512]{3,0,2,1:T(8,128)(2,1)}) fusion(bf16[32,8,32,512]{3,0,2,1:T(8,128)(2,1)} %bitcast.79), kind=kLoop, calls=%fused_computation.83 | loop fusion | bytes 16777216 | tf_op jit(solution)/shard_map/split | solution.py:36
  145.4 4.3 copy.91
  149.7 5.6 %all-to-all-start.2 = ((bf16[32,8,16,512]{3,2,1,0:T(8,128)(2,1)}), bf16[32,8,16,512]{3,2,1,0:T(8,128)(2,1)}, u32[]{:S(2)}, u32[]{:S(2)}) async-start(bf16[32,8,16,512]{3,2,1,0:T(8,128)(2,1)} %copy.91), calls=%async_computation.2 | async-start | bytes 8388608 | tf_op jit(solution)/shard_map/all_to_all | solution.py:38
  155.3 6.5 %copy.92 = bf16[32,8,16,512]{3,2,1,0:T(8,128)(2,1)} copy(bf16[32,8,16,512]{3,0,2,1:T(8,128)(2,1)} %get-tuple-element.8) | data formatting | bytes 8388608 | tf_op jit(solution)/shard_map/split | solution.py:36
  161.8 85.3 %all-to-all-done.2 = bf16[32,8,16,512]{3,2,1,0:T(8,128)(2,1)} async-done(((bf16[32,8,16,512]{3,2,1,0:T(8,128)(2,1)}), bf16[32,8,16,512]{3,2,1,0:T(8,128)(2,1)}, u32[]{:S(2)}, u32[]{:S(2)}) %all-to-all-start.2) | async-done | bytes 4194336 | tf_op jit(solution)/shard_map/all_to_all | solution.py:38
  247.2 8.4 %all-to-all-start.3 = ((bf16[32,8,16,512]{3,2,1,0:T(8,128)(2,1)}), bf16[32,8,16,512]{3,2,1,0:T(8,128)(2,1)}, u32[]{:S(2)}, u32[]{:S(2)}) async-start(bf16[32,8,16,512]{3,2,1,0:T(8,128)(2,1)} %copy.92), calls=%async_computation.3 | async-start | bytes 8388608 | tf_op jit(solution)/shard_map/all_to_all | solution.py:38
  255.6 0.0 reduce-scatter.2.cloned.1.call-start
  255.7 0.0 copy-done
  255.7 2.1 gather_fusion.1
  257.8 90.0 %all-to-all-done.3 = bf16[32,8,16,512]{3,2,1,0:T(8,128)(2,1)} async-done(((bf16[32,8,16,512]{3,2,1,0:T(8,128)(2,1)}), bf16[32,8,16,512]{3,2,1,0:T(8,128)(2,1)}, u32[]{:S(2)}, u32[]{:S(2)}) %all-to-all-start.3) | async-done | bytes 4194336 | tf_op jit(solution)/shard_map/all_to_all | solution.py:38
  347.8 8.2 %maximum_bitcast_fusion = bf16[8,32,32,512]{3,2,0,1:T(8,128)(2,1)} fusion(bf16[32,8,16,512]{3,2,1,0:T(8,128)(2,1)} %all-to-all-done.3, bf16[32,8,16,512]{3,2,1,0:T(8,128)(2,1)} %all-to-all-done.2), kind=kLoop, calls=%fused_computation.8 | loop fusion | flops 16777216 | bytes 16777216 | tf_op jit(solution)/shard_map/transpose | solution.py:29
  356.0 8.4 %copy.93 = bf16[8,32,32,512]{3,2,1,0:T(8,128)(2,1)} copy(bf16[8,32,32,512]{3,2,0,1:T(8,128)(2,1)} %maximum_bitcast_fusion) | data formatting | bytes 16777216 | tf_op jit(solution)/shard_map/transpose | solution.py:29
  364.5 0.0 copy-done.2
  364.5 9.1 %convert_bitcast_fusion = bf16[8,512,8,128]{1,3,2,0:T(8,128)(2,1)} fusion(bf16[8,8,128,512]{3,2,1,0:T(8,128)(2,1)} %bitcast.77, bf16[8,8,128,128]{3,2,1,0:T(8,128)(2,1)S(1)} %copy-done.2, pred[8]{0:T(512)(128)(4,1)S(1)} %compare_and_fusion.2), kind=kOutput, calls=%fused_computation.14 | convolution fusion | flops 1078984704 | bytes 18874376 | tf_op jit(solution)/shard_map/dtkr,dtkj->drtj/dot_general | solution.py:102
  373.5 12.7 %copy.95 = bf16[8,512,8,128]{3,2,1,0:T(8,128)(2,1)} copy(bf16[8,512,8,128]{1,3,2,0:T(8,128)(2,1)} %convert_bitcast_fusion) | data formatting | bytes 16777216 | tf_op jit(solution)/shard_map/convert_element_type | solution.py:104
  386.2 8.8 %copy.116 = bf16[512,8,8,128]{3,1,2,0:T(8,128)(2,1)} copy(bf16[512,8,8,128]{3,2,1,0:T(8,128)(2,1)} %bitcast.80) | data formatting | bytes 16777216
  395.0 0.0 reduce-scatter.2.cloned.1.call-update
  395.0 0.7 copy-done.5
  395.7 0.1 copy.76
  395.8 0.1 reshape.82
  395.9 0.1 copy.72
  396.0 0.1 copy.71
  396.1 0.1 copy.73
  396.2 9.9 %gather_fusion = bf16[1024,32,128]{2,1,0:T(8,128)(2,1)} fusion(bf16[32,128,128]{2,0,1:T(8,128)(2,1)S(1)} %copy.77, s32[1024]{0:T(1024)S(1)} %broadcast_clamp_fusion.1), kind=kCustom, calls=%fused_computation | custom fusion | bytes 16781312 | tf_op jit(solution)/shard_map/jit(_take)/gather | solution.py:66
  406.1 7.2 %convert_bitcast_fusion.2 = bf16[32,128,8,128]{3,2,0,1:T(8,128)(2,1)S(1)} fusion(bf16[128,8,32,128]{3,2,1,0:T(8,128)(2,1)} %bitcast.81, pred[128,8]{1,0:T(8,128)(4,1)S(1)} %copy.73, s32[128,8]{1,0:T(8,128)S(1)} %copy.72, s32[128,8]{1,0:T(8,128)S(1)} %copy.71), kind=kOutput, calls=%fused_computation.16 | convolution fusion | flops 75522048 | bytes 16786432 | tf_op jit(solution)/shard_map/cpki,pkg->cpgi/dot_general | solution.py:72
  413.3 6.1 %bitcast_convert_fusion = bf16[32,128,128]{2,1,0:T(8,128)(2,1)} fusion(bf16[32,128,8,128]{3,2,0,1:T(8,128)(2,1)S(1)} %convert_bitcast_fusion.2, bf16[8,128,128]{2,1,0:T(8,128)(2,1)S(1)} %copy-done.10), kind=kOutput, calls=%fused_computation.21 | convolution fusion | flops 1074266112 | bytes 9699328 | tf_op jit(solution)/shard_map/cpgj,gij->cpi/dot_general | solution.py:75
  419.4 1.7 convert_element_type.53
  421.1 0.6 copy.80
  421.7 0.0 copy-start.3
  421.7 34.0 %all_to_all.36 = bf16[32,32,512]{2,0,1:T(8,128)(2,1)S(1)} all-to-all(bf16[32,32,512]{2,0,1:T(8,128)(2,1)S(1)} %copy.80), channel_id=1, replica_groups=mesh['sym'=8,'rows'=32] {'rows'}, dimensions={1} | all-to-all | bytes 2097152 | tf_op jit(solution)/shard_map/all_to_all | solution.py:78
  455.8 1.6 transpose.48
  457.4 3.0 copy.81
  460.3 0.0 copy-done.3
  460.3 5.1 %fusion.12 = f32[512,1024]{1,0:T(8,128)} fusion(f32[1024,512]{0,1:T(8,128)} %copy.81, bf16[512,1024]{1,0:T(8,128)(2,1)} %reduce-scatter.2.cloned.1.call-done, bf16[512,1024]{1,0:T(8,128)(2,1)S(1)} %copy-done.3, bf16[1,1024,1024]{2,1,0:T(8,128)(2,1)} %param.12), kind=kOutput, calls=%fused_computation.20 | convolution fusion | flops 1075314688 | bytes 8388608 | tf_op jit(solution)/shard_map/dot_general | solution.py:62
  (22 shorter events, 0.1 us)
Async XLA Ops:
  6.5 249.1 %copy-start = (bf16[1,8,8,128,128]{4,3,2,1,0:T(8,128)(2,1)S(1)}, bf16[1,8,8,128,128]{4,3,2,1,0:T(8,128)(2,1)}, u32[]{:S(2)}) copy-start(bf16[1,8,8,128,128]{4,3,2,1,0:T(8,128)(2,1)} %param.13) | copy-start | bytes 6291460
  6.5 15.0 %copy-start.1 = (s32[32,32,2]{1,2,0:T(2,128)S(1)}, s32[32,32,2]{1,2,0:T(2,128)}, u32[]{:S(2)}) copy-start(s32[32,32,2]{1,2,0:T(2,128)} %param.15) | copy-start | bytes 24580
  9.0 39.7 %all-to-all-start = ((bf16[32,32,512]{2,1,0:T(8,128)(2,1)}), bf16[32,32,512]{2,1,0:T(8,128)(2,1)S(1)}, u32[]{:S(2)}, u32[]{:S(2)}) async-start(bf16[32,32,512]{2,1,0:T(8,128)(2,1)} %bitcast.84), calls=%async_computation | async-start | bytes 2097152 | tf_op jit(solution)/shard_map/all_to_all | solution.py:64
  21.5 20.3 %copy-start.4 = (s32[128,16]{0,1:T(8,128)S(1)}, s32[128,16]{0,1:T(8,128)}, u32[]{:S(2)}) copy-start(s32[128,16]{0,1:T(8,128)} %param.16) | copy-start | bytes 24580
  21.5 20.6 %copy-start.6 = (s32[128,16]{0,1:T(8,128)S(1)}, s32[128,16]{0,1:T(8,128)}, u32[]{:S(2)}) copy-start(s32[128,16]{0,1:T(8,128)} %param.18) | copy-start | bytes 24580
  21.5 20.7 %copy-start.7 = (s32[128,16]{0,1:T(8,128)S(1)}, s32[128,16]{0,1:T(8,128)}, u32[]{:S(2)}) copy-start(s32[128,16]{0,1:T(8,128)} %param.17) | copy-start | bytes 24580
  149.7 97.5 %all-to-all-start.2 = ((bf16[32,8,16,512]{3,2,1,0:T(8,128)(2,1)}), bf16[32,8,16,512]{3,2,1,0:T(8,128)(2,1)}, u32[]{:S(2)}, u32[]{:S(2)}) async-start(bf16[32,8,16,512]{3,2,1,0:T(8,128)(2,1)} %copy.91), calls=%async_computation.2 | async-start | bytes 8388608 | tf_op jit(solution)/shard_map/all_to_all | solution.py:38
  247.2 100.6 %all-to-all-start.3 = ((bf16[32,8,16,512]{3,2,1,0:T(8,128)(2,1)}), bf16[32,8,16,512]{3,2,1,0:T(8,128)(2,1)}, u32[]{:S(2)}, u32[]{:S(2)}) async-start(bf16[32,8,16,512]{3,2,1,0:T(8,128)(2,1)} %copy.92), calls=%async_computation.3 | async-start | bytes 8388608 | tf_op jit(solution)/shard_map/all_to_all | solution.py:38
  255.6 204.7 %reduce-scatter.2.cloned.1.call-start = ((), (), s32[]{:S(2)}) async-start(), calls=%async_computation.5 | async-start | bytes 9437184 | tf_op jit(solution)/shard_map/reduce_scatter | solution.py:103
  356.0 8.4 %copy-start.2 = (bf16[8,8,128,128]{3,2,1,0:T(8,128)(2,1)S(1)}, bf16[8,8,128,128]{3,2,1,0:T(8,128)(2,1)}, u32[]{:S(2)}) copy-start(bf16[8,8,128,128]{3,2,1,0:T(8,128)(2,1)} %gather_fusion.1) | copy-start | bytes 6291460
  395.0 0.7 copy-start.5
  395.0 0.9 copy-start.9
  395.0 1.0 copy-start.8
  406.1 7.2 %copy-start.10 = (bf16[8,128,128]{2,1,0:T(8,128)(2,1)S(1)}, bf16[8,128,128]{2,1,0:T(8,128)(2,1)}, u32[]{:S(2)}) copy-start(bf16[8,128,128]{2,1,0:T(8,128)(2,1)} %param.14) | copy-start | bytes 786436
  421.7 38.6 %copy-start.3 = (bf16[512,1024]{1,0:T(8,128)(2,1)S(1)}, bf16[512,1024]{1,0:T(8,128)(2,1)}, u32[]{:S(2)}) copy-start(bf16[512,1024]{1,0:T(8,128)(2,1)} %param.11) | copy-start | bytes 3145732
Sparse Core Ops, SparseCore 0:
  395.1 51.5 reduce-scatter.1
where the time goes:
time: 480 us; the launch traced here: 473 us
  waiting for transfers between devices  182 us (38%)
  local copies, waits for them, and re-layouts  139 us (29%)
  matrix products  53.3 us (11%)
  blocking collectives  34 us (7%)
  starting transfers between devices  25.7 us (5%)
  other arithmetic  25 us (5%)
  between operations  14 us (3%)
    all_to_all x2, waiting for transfers between devices, exchange_in_pieces(): lax.all_to_all(slab, axis, split_axis=0, concat_axis=0, tiled=True)  175 us
    all_to_all x1, blocking collectives, per_device(): lax.all_to_all(alpha_part.astype(jnp.bfloat16), 'rows', split_axis=1, con...  34 us
    dot_general x1, matrix products, per_device(): jnp.einsum('cpli,dpl->dcpi', gathered, mix_weight, preferred_element_type...  25.9 us
    gather x3, local copies, waits for them, and re-layouts, per_device(): owned_blk = send_list[slot_src, dest_rank, slot_pos]  20.2 us
    gather x1, local copies, waits for them, and re-layouts, per_device(): gathered = jnp.take(col_blocks, source, axis=1)  19.2 us
    split x3, local copies, waits for them, and re-layouts, exchange_in_pieces(): jnp.split(parts, piece_ends(parts.shape[widest], pieces), axis=widest)  16.1 us
    select_n x1, other arithmetic, per_device(): gathered = jnp.take(col_blocks, source, axis=1)  14.4 us
    all_to_all x2, starting transfers between devices, exchange_in_pieces(): lax.all_to_all(slab, axis, split_axis=0, concat_axis=0, tiled=True)  14 us
  transfers between devices with their start and end apart: 4, of which 3 were waited for; matrix products, arithmetic and copies ran while one was open for 13% of the time, Pallas kernels for 0%

commit v1 on v0

--- a/solution.py
+++ b/solution.py
@@ -75,8 +75,14 @@
     alpha_part = jnp.einsum(
         "cpgj,gij->cpi", combined, pair_op, preferred_element_type=jnp.float32
     ).reshape(col_width, total_rows)
-    returned = lax.all_to_all(
-        alpha_part.astype(jnp.bfloat16), "rows", split_axis=1, concat_axis=0, tiled=True
+    returned = jnp.concatenate(
+        lax.all_to_all(
+            jnp.stack(jnp.split(alpha_part.astype(jnp.bfloat16), lax.axis_size("rows"), axis=1)),
+            "rows",
+            0,
+            0,
+        ),
+        axis=0,
     ).astype(alpha_part.dtype)
     dest_ids = jnp.arange(sectors, dtype=jnp.int32)
     pair_of = jnp.bitwise_xor(sector, dest_ids)

time: 480 us -> 478 us (level)
    unnamed x26 -> x58, local copies, waits for them, and re-layouts: 12.1 us -> 12.9 us
  transfers between devices with their start and end apart: 4 -> 4, of which waited for: 3 -> 3; matrix products, arithmetic and copies ran while one was open for 13% -> 12% of each run, Pallas kernels for 0% -> 0%
where the time goes in v1:
time: 478 us; the launch traced here: 470 us
  waiting for transfers between devices  182 us (38%)
  local copies, waits for them, and re-layouts  138 us (29%)
  matrix products  52.3 us (11%)
  blocking collectives  33.9 us (7%)
  starting transfers between devices  25.7 us (5%)
  other arithmetic  25.1 us (5%)
  between operations  14.3 us (3%)
    all_to_all x2, waiting for transfers between devices, exchange_in_pieces(): lax.all_to_all(slab, axis, split_axis=0, concat_axis=0, tiled=True)  175 us
    all_to_all x1, blocking collectives, per_device(): lax.all_to_all(jnp.stack(jnp.split(alpha_part.astype(jnp.bfloat16), lax.a...  33.9 us
    dot_general x1, matrix products, per_device(): jnp.einsum('cpli,dpl->dcpi', gathered, mix_weight, preferred_element_type...  25.9 us
    gather x3, local copies, waits for them, and re-layouts, per_device(): owned_blk = send_list[slot_src, dest_rank, slot_pos]  20.2 us
    gather x1, local copies, waits for them, and re-layouts, per_device(): gathered = jnp.take(col_blocks, source, axis=1)  19.2 us
    split x3, local copies, waits for them, and re-layouts, exchange_in_pieces(): jnp.split(parts, piece_ends(parts.shape[widest], pieces), axis=widest)  16.1 us
    select_n x1, other arithmetic, per_device(): gathered = jnp.take(col_blocks, source, axis=1)  14.4 us
    all_to_all x2, starting transfers between devices, exchange_in_pieces(): lax.all_to_all(slab, axis, split_axis=0, concat_axis=0, tiled=True)  14 us
  transfers between devices with their start and end apart: 4, of which 3 were waited for; matrix products, arithmetic and copies ran while one was open for 12% of the time, Pallas kernels for 0%

profile of v1, /device:TPU:18, one launch (start us, length us, event | category | flops | bytes accessed | tf_op | source)
XLA Modules:
  0.0 470.4 jit_solution(17785702080116994374)
XLA Ops:
  6.5 0.0 copy-start
  6.5 2.4 copy.103
  9.0 11.6 %all-to-all-start = ((bf16[32,32,512]{2,1,0:T(8,128)(2,1)}), bf16[32,32,512]{2,1,0:T(8,128)(2,1)S(1)}, u32[]{:S(2)}, u32[]{:S(2)}) async-start(bf16[32,32,512]{2,1,0:T(8,128)(2,1)} %bitcast.247), calls=%async_computation | async-start | bytes 2097152 | tf_op jit(solution)/shard_map/all_to_all | solution.py:64
  20.6 0.7 fusion.38
  21.3 0.1 copy.112
  21.4 0.1 reshape.93
  21.5 0.0 copy-done.1
  21.5 0.0 copy-start.4
  21.5 0.0 copy-start.6
  21.5 0.0 copy-start.7
  21.5 20.1 %gather_fusion.2 = s32[2048]{0:T(1024)S(1)} fusion(s32[32,32,2]{1,2,0:T(2,128)S(1)} %copy-done.1, s32[2048]{0:T(1024)S(1)} %reshape.93), kind=kCustom, calls=%fused_computation.2 | custom fusion | bytes 40960 | tf_op jit(solution)/shard_map/gather | solution.py:94
  41.7 0.1 reshape.96
  41.7 0.1 copy.113
  41.8 0.0 copy-done.4
  41.8 0.1 copy.115
  41.9 0.1 reshape.101
  42.0 0.1 copy.114
  42.2 0.0 copy-done.6
  42.2 0.1 copy.110
  42.3 0.0 copy-done.7
  42.3 0.1 copy.111
  42.4 6.2 %all-to-all-done = bf16[32,32,512]{2,1,0:T(8,128)(2,1)S(1)} async-done(((bf16[32,32,512]{2,1,0:T(8,128)(2,1)}), bf16[32,32,512]{2,1,0:T(8,128)(2,1)S(1)}, u32[]{:S(2)}, u32[]{:S(2)}) %all-to-all-start) | async-done | bytes 1048608 | tf_op jit(solution)/shard_map/all_to_all | solution.py:64
  48.7 1.5 copy.104
  50.2 2.5 reshape.75
  52.7 1.9 copy.106
  54.6 19.2 %gather_fusion.3 = bf16[2048,32,128]{2,1,0:T(8,128)(2,1)} fusion(bf16[32,128,128]{2,0,1:T(8,128)(2,1)S(1)} %copy.106, s32[2048]{0:T(1024)S(1)} %broadcast_clamp_fusion), kind=kCustom, calls=%fused_computation.3 | custom fusion | bytes 33562624 | tf_op jit(solution)/shard_map/jit(_take)/gather | solution.py:96
  73.8 14.4 %select_bitcast_fusion = bf16[32,128,16,128]{3,0,2,1:T(8,128)(2,1)} fusion(bf16[128,16,32,128]{3,2,1,0:T(8,128)(2,1)} %bitcast.208, pred[128,16]{1,0:T(8,128)(4,1)S(1)} %copy.114), kind=kLoop, calls=%fused_computation.6 | loop fusion | flops 8388608 | bytes 33556480 | tf_op jit(solution)/shard_map/jit(_take)/select_n | solution.py:96
  88.2 25.9 %convert_bitcast_fusion.1 = bf16[8,32,128,128]{3,0,1,2:T(8,128)(2,1)} fusion(bf16[32,128,16,128]{3,0,2,1:T(8,128)(2,1)} %select_bitcast_fusion, bf16[128,16]{1,0:T(8,128)(2,1)S(1)} %copy.111, s32[128,16]{1,0:T(8,128)S(1)} %copy.110, s32[8]{0:T(128)S(1)} %iota_xor_fusion), kind=kOutput, calls=%fused_computation.15 | convolution fusion | flops 138444800 | bytes 25178144 | tf_op jit(solution)/shard_map/cpli,dpl->dcpi/dot_general | solution.py:100
  114.1 12.0 %copy.118 = bf16[8,32,128,128]{3,2,1,0:T(8,128)(2,1)} copy(bf16[8,32,128,128]{3,0,1,2:T(8,128)(2,1)} %convert_bitcast_fusion.1) | data formatting | bytes 16777216 | tf_op jit(solution)/shard_map/convert_element_type | solution.py:102
  126.1 14.0 %reshape_reshape.6 = bf16[8,32,32,512]{3,2,1,0:T(8,128)(2,1)} reshape(bf16[8,32,128,128]{3,2,1,0:T(8,128)(2,1)} %copy.118) | data formatting | bytes 16777216 | tf_op jit(solution)/shard_map/reshape;reshape | solution.py:15
  140.1 5.3 %fusion.51 = (bf16[32,8,16,512]{3,0,2,1:T(8,128)(2,1)S(1)}, bf16[32,8,16,512]{3,0,2,1:T(8,128)(2,1)}) fusion(bf16[32,8,32,512]{3,0,2,1:T(8,128)(2,1)} %bitcast.211), kind=kLoop, calls=%fused_computation.149 | loop fusion | bytes 16777216 | tf_op jit(solution)/shard_map/split | solution.py:36
  145.4 4.3 copy.119
  149.7 5.6 %all-to-all-start.2 = ((bf16[32,8,16,512]{3,2,1,0:T(8,128)(2,1)}), bf16[32,8,16,512]{3,2,1,0:T(8,128)(2,1)}, u32[]{:S(2)}, u32[]{:S(2)}) async-start(bf16[32,8,16,512]{3,2,1,0:T(8,128)(2,1)} %copy.119), calls=%async_computation.2 | async-start | bytes 8388608 | tf_op jit(solution)/shard_map/all_to_all | solution.py:38
  155.3 6.5 %copy.120 = bf16[32,8,16,512]{3,2,1,0:T(8,128)(2,1)} copy(bf16[32,8,16,512]{3,0,2,1:T(8,128)(2,1)} %get-tuple-element.8) | data formatting | bytes 8388608 | tf_op jit(solution)/shard_map/split | solution.py:36
  161.8 85.3 %all-to-all-done.2 = bf16[32,8,16,512]{3,2,1,0:T(8,128)(2,1)} async-done(((bf16[32,8,16,512]{3,2,1,0:T(8,128)(2,1)}), bf16[32,8,16,512]{3,2,1,0:T(8,128)(2,1)}, u32[]{:S(2)}, u32[]{:S(2)}) %all-to-all-start.2) | async-done | bytes 4194336 | tf_op jit(solution)/shard_map/all_to_all | solution.py:38
  247.2 8.4 %all-to-all-start.3 = ((bf16[32,8,16,512]{3,2,1,0:T(8,128)(2,1)}), bf16[32,8,16,512]{3,2,1,0:T(8,128)(2,1)}, u32[]{:S(2)}, u32[]{:S(2)}) async-start(bf16[32,8,16,512]{3,2,1,0:T(8,128)(2,1)} %copy.120), calls=%async_computation.3 | async-start | bytes 8388608 | tf_op jit(solution)/shard_map/all_to_all | solution.py:38
  255.6 0.0 reduce-scatter.2.cloned.1.call-start
  255.7 0.0 copy-done
  255.7 2.1 gather_fusion.1
  257.8 90.0 %all-to-all-done.3 = bf16[32,8,16,512]{3,2,1,0:T(8,128)(2,1)} async-done(((bf16[32,8,16,512]{3,2,1,0:T(8,128)(2,1)}), bf16[32,8,16,512]{3,2,1,0:T(8,128)(2,1)}, u32[]{:S(2)}, u32[]{:S(2)}) %all-to-all-start.3) | async-done | bytes 4194336 | tf_op jit(solution)/shard_map/all_to_all | solution.py:38
  347.8 8.2 %maximum_bitcast_fusion = bf16[8,32,32,512]{3,2,0,1:T(8,128)(2,1)} fusion(bf16[32,8,16,512]{3,2,1,0:T(8,128)(2,1)} %all-to-all-done.3, bf16[32,8,16,512]{3,2,1,0:T(8,128)(2,1)} %all-to-all-done.2), kind=kLoop, calls=%fused_computation.8 | loop fusion | flops 16777216 | bytes 16777216 | tf_op jit(solution)/shard_map/transpose | solution.py:29
  356.0 8.4 %copy.121 = bf16[8,32,32,512]{3,2,1,0:T(8,128)(2,1)} copy(bf16[8,32,32,512]{3,2,0,1:T(8,128)(2,1)} %maximum_bitcast_fusion) | data formatting | bytes 16777216 | tf_op jit(solution)/shard_map/transpose | solution.py:29
  364.5 0.0 copy-done.2
  364.5 9.1 %convert_bitcast_fusion = bf16[8,512,8,128]{1,3,2,0:T(8,128)(2,1)} fusion(bf16[8,8,128,512]{3,2,1,0:T(8,128)(2,1)} %bitcast.209, bf16[8,8,128,128]{3,2,1,0:T(8,128)(2,1)S(1)} %copy-done.2, pred[8]{0:T(512)(128)(4,1)S(1)} %compare_and_fusion.2), kind=kOutput, calls=%fused_computation.14 | convolution fusion | flops 1078984704 | bytes 18874376 | tf_op jit(solution)/shard_map/dtkr,dtkj->drtj/dot_general | solution.py:108
  373.5 12.7 %copy.123 = bf16[8,512,8,128]{3,2,1,0:T(8,128)(2,1)} copy(bf16[8,512,8,128]{1,3,2,0:T(8,128)(2,1)} %convert_bitcast_fusion) | data formatting | bytes 16777216 | tf_op jit(solution)/shard_map/convert_element_type | solution.py:110
  386.2 8.8 %copy.146 = bf16[512,8,8,128]{3,1,2,0:T(8,128)(2,1)} copy(bf16[512,8,8,128]{3,2,1,0:T(8,128)(2,1)} %bitcast.212) | data formatting | bytes 16777216
  395.0 0.0 reduce-scatter.2.cloned.1.call-update
  395.0 0.7 copy-done.5
  395.7 0.1 copy.105
  395.8 0.1 reshape.79
  395.8 0.0 copy-done.9
  395.9 0.1 copy.101
  396.0 0.0 copy-done.8
  396.0 0.1 copy.100
  396.1 0.1 copy.102
  396.2 9.9 %gather_fusion = bf16[1024,32,128]{2,1,0:T(8,128)(2,1)} fusion(bf16[32,128,128]{2,0,1:T(8,128)(2,1)S(1)} %copy.106, s32[1024]{0:T(1024)S(1)} %broadcast_clamp_fusion.1), kind=kCustom, calls=%fused_computation | custom fusion | bytes 16781312 | tf_op jit(solution)/shard_map/jit(_take)/gather | solution.py:66
  406.1 7.2 %convert_bitcast_fusion.2 = bf16[32,128,8,128]{3,2,0,1:T(8,128)(2,1)S(1)} fusion(bf16[128,8,32,128]{3,2,1,0:T(8,128)(2,1)} %bitcast.213, pred[128,8]{1,0:T(8,128)(4,1)S(1)} %copy.102, s32[128,8]{1,0:T(8,128)S(1)} %copy.101, s32[128,8]{1,0:T(8,128)S(1)} %copy.100), kind=kOutput, calls=%fused_computation.16 | convolution fusion | flops 75522048 | bytes 16786432 | tf_op jit(solution)/shard_map/cpki,pkg->cpgi/dot_general | solution.py:72
  413.3 5.1 %bitcast_convert_fusion = bf16[32,128,128]{2,1,0:T(8,128)(2,1)S(1)} fusion(bf16[32,128,8,128]{3,2,0,1:T(8,128)(2,1)S(1)} %convert_bitcast_fusion.2, bf16[8,128,128]{2,1,0:T(8,128)(2,1)S(1)} %copy-done.10), kind=kOutput, calls=%fused_computation.21 | convolution fusion | flops 1074266112 | bytes 9699328 | tf_op jit(solution)/shard_map/cpgj,gij->cpi/dot_general | solution.py:75
  418.4 0.0 copy-start.3
  418.5 0.7 copy.147
  419.5 33.9 %all_to_all.31 = bf16[32,32,512]{2,1,0:T(8,128)(2,1)S(1)} all-to-all(bf16[32,32,512]{2,1,0:T(8,128)(2,1)S(1)} %constant_dynamic-update-slice_fusion), channel_id=1, replica_groups=mesh['sym'=8,'rows'=32] {'rows'}, dimensions={0} | all-to-all | bytes 2097152 | tf_op jit(solution)/shard_map/all_to_all | solution.py:79
  453.4 1.7 bitcast_convert_fusion.1
  455.1 3.0 copy.109
  458.1 5.1 %fusion.12 = f32[512,1024]{1,0:T(8,128)} fusion(f32[1024,512]{0,1:T(8,128)} %copy.109, bf16[512,1024]{1,0:T(8,128)(2,1)} %reduce-scatter.2.cloned.1.call-done, bf16[512,1024]{1,0:T(8,128)(2,1)S(1)} %copy-done.3, bf16[1,1024,1024]{2,1,0:T(8,128)(2,1)} %param.12), kind=kOutput, calls=%fused_computation.20 | convolution fusion | flops 1075314688 | bytes 8388608 | tf_op jit(solution)/shard_map/dot_general | solution.py:62
  (53 shorter events, 0.3 us)
Async XLA Ops:
  6.5 249.1 %copy-start = (bf16[1,8,8,128,128]{4,3,2,1,0:T(8,128)(2,1)S(1)}, bf16[1,8,8,128,128]{4,3,2,1,0:T(8,128)(2,1)}, u32[]{:S(2)}) copy-start(bf16[1,8,8,128,128]{4,3,2,1,0:T(8,128)(2,1)} %param.13) | copy-start | bytes 6291460
  6.5 15.0 %copy-start.1 = (s32[32,32,2]{1,2,0:T(2,128)S(1)}, s32[32,32,2]{1,2,0:T(2,128)}, u32[]{:S(2)}) copy-start(s32[32,32,2]{1,2,0:T(2,128)} %param.15) | copy-start | bytes 24580
  9.0 39.7 %all-to-all-start = ((bf16[32,32,512]{2,1,0:T(8,128)(2,1)}), bf16[32,32,512]{2,1,0:T(8,128)(2,1)S(1)}, u32[]{:S(2)}, u32[]{:S(2)}) async-start(bf16[32,32,512]{2,1,0:T(8,128)(2,1)} %bitcast.247), calls=%async_computation | async-start | bytes 2097152 | tf_op jit(solution)/shard_map/all_to_all | solution.py:64
  21.5 20.3 %copy-start.4 = (s32[128,16]{0,1:T(8,128)S(1)}, s32[128,16]{0,1:T(8,128)}, u32[]{:S(2)}) copy-start(s32[128,16]{0,1:T(8,128)} %param.16) | copy-start | bytes 24580
  21.5 20.6 %copy-start.6 = (s32[128,16]{0,1:T(8,128)S(1)}, s32[128,16]{0,1:T(8,128)}, u32[]{:S(2)}) copy-start(s32[128,16]{0,1:T(8,128)} %param.18) | copy-start | bytes 24580
  21.5 20.7 %copy-start.7 = (s32[128,16]{0,1:T(8,128)S(1)}, s32[128,16]{0,1:T(8,128)}, u32[]{:S(2)}) copy-start(s32[128,16]{0,1:T(8,128)} %param.17) | copy-start | bytes 24580
  149.7 97.5 %all-to-all-start.2 = ((bf16[32,8,16,512]{3,2,1,0:T(8,128)(2,1)}), bf16[32,8,16,512]{3,2,1,0:T(8,128)(2,1)}, u32[]{:S(2)}, u32[]{:S(2)}) async-start(bf16[32,8,16,512]{3,2,1,0:T(8,128)(2,1)} %copy.119), calls=%async_computation.2 | async-start | bytes 8388608 | tf_op jit(solution)/shard_map/all_to_all | solution.py:38
  247.2 100.6 %all-to-all-start.3 = ((bf16[32,8,16,512]{3,2,1,0:T(8,128)(2,1)}), bf16[32,8,16,512]{3,2,1,0:T(8,128)(2,1)}, u32[]{:S(2)}, u32[]{:S(2)}) async-start(bf16[32,8,16,512]{3,2,1,0:T(8,128)(2,1)} %copy.120), calls=%async_computation.3 | async-start | bytes 8388608 | tf_op jit(solution)/shard_map/all_to_all | solution.py:38
  255.6 202.5 %reduce-scatter.2.cloned.1.call-start = ((), (), s32[]{:S(2)}) async-start(), calls=%async_computation.5 | async-start | bytes 9437184 | tf_op jit(solution)/shard_map/reduce_scatter | solution.py:109
  356.0 8.4 %copy-start.2 = (bf16[8,8,128,128]{3,2,1,0:T(8,128)(2,1)S(1)}, bf16[8,8,128,128]{3,2,1,0:T(8,128)(2,1)}, u32[]{:S(2)}) copy-start(bf16[8,8,128,128]{3,2,1,0:T(8,128)(2,1)} %gather_fusion.1) | copy-start | bytes 6291460
  395.0 0.7 copy-start.5
  395.0 0.9 copy-start.9
  395.0 1.0 copy-start.8
  406.1 7.2 %copy-start.10 = (bf16[8,128,128]{2,1,0:T(8,128)(2,1)S(1)}, bf16[8,128,128]{2,1,0:T(8,128)(2,1)}, u32[]{:S(2)}) copy-start(bf16[8,128,128]{2,1,0:T(8,128)(2,1)} %param.14) | copy-start | bytes 786436
  418.4 39.6 %copy-start.3 = (bf16[512,1024]{1,0:T(8,128)(2,1)S(1)}, bf16[512,1024]{1,0:T(8,128)(2,1)}, u32[]{:S(2)}) copy-start(bf16[512,1024]{1,0:T(8,128)(2,1)} %param.11) | copy-start | bytes 3145732
Sparse Core Ops, SparseCore 0:
  395.1 51.5 reduce-scatter.1
